TPU v7x, 32 devices: a whole 2x2x4 slice. The times are simulated.
32 devices in a mesh: inner: 4 (over y, x), blk: 8 (over z, core).
Axes of the slice: x: 2, y: 2, z: 4, core: 2. Of those that a mesh axis runs over, the one named last changes fastest.
Arguments:
- image_emb: float32 [768, 768], P(('inner', 'blk')), may hold values from -150 to 150
- text_emb: float32 [768, 768], P(('inner', 'blk')), may hold values from -150 to 150
- logit_scale: float32 [1], replicated, may hold values from 30 to 100
Outputs:
- mean_loss: float32 [1], replicated
- image_grad: float32 [768, 768], P(('inner', 'blk'))
- text_grad: float32 [768, 768], P(('inner', 'blk'))
All inputs are finite; a program needn't handle non-finite values.
Results may differ from a plain program's by a relative error of at most 0.006.
Values may be sent and summed in bfloat16 or wider, within the bound.
A program may use at most 64 MiB of HBM per device.

v0:
```python
import functools

import jax
import jax.numpy as jnp
from jax import lax
from jax.experimental import pallas as pl
from jax.experimental.pallas import tpu as pltpu
from jax.sharding import PartitionSpec as P

EPSILON = 1e-06
MESH = pl.DeviceIdType.MESH


def unit_rows(values):
    inverse = lax.rsqrt(jnp.sum(values * values, axis=1, keepdims=True) + EPSILON)
    return (values * inverse, inverse)


def project(gradient, direction, inverse):
    return (gradient - direction * jnp.sum(gradient * direction, axis=1, keepdims=True)) * inverse


class Group:
    def __init__(self, me, size, device_of, sems):
        self.me, self.size, self.device_of, self.sems = me, size, device_of, sems

    def on(self, step):
        return lax.rem(self.me + step, self.size)

    def back(self, step):
        return lax.rem(self.me + self.size - step, self.size)

    def copy(self, src, dst, stage, step, to):
        send_sems, recv_sems = self.sems
        return pltpu.make_async_remote_copy(
            src_ref=src,
            dst_ref=dst,
            send_sem=send_sems.at[stage, step],
            recv_sem=recv_sems.at[stage, step],
            device_id=self.device_of(to),
            device_id_type=MESH,
        )

    def steps(self):
        return range(1, self.size)

    def start_gather(self, buf, stage):
        mine = buf.at[self.me]
        for step in self.steps():
            self.copy(mine, mine, stage, step, self.on(step)).start()

    def wait_gather(self, buf, stage):
        for step in self.steps():
            theirs = buf.at[self.back(step)]
            self.copy(theirs, theirs, stage, step, self.back(step)).wait_recv()

    def end_gather(self, buf, stage):
        mine = buf.at[self.me]
        for step in self.steps():
            self.copy(mine, mine, stage, step, self.on(step)).wait_send()

    def start_scatter(self, parts, slots, stage):
        for step in self.steps():
            to = self.on(step)
            self.copy(parts.at[to], slots.at[step], stage, step, to).start()

    def wait_scatter(self, parts, slots, stage):
        for step in self.steps():
            to = self.on(step)
            self.copy(parts.at[to], slots.at[step], stage, step, to).wait()


def as_column(row):
    size = row.shape[1]
    shape = (size, size)
    same = lax.broadcasted_iota(jnp.int32, shape, 0) == lax.broadcasted_iota(jnp.int32, shape, 1)
    return jnp.sum(jnp.where(same, row, 0.0), axis=1, keepdims=True)


def as_row(column):
    size = column.shape[0]
    shape = (size, size)
    same = lax.broadcasted_iota(jnp.int32, shape, 0) == lax.broadcasted_iota(jnp.int32, shape, 1)
    return jnp.sum(jnp.where(same, column, 0.0), axis=0, keepdims=True)


def merge(stats):
    highest = jnp.max(stats[:, 0:1, :], axis=0)
    total = jnp.sum(stats[:, 1:2, :] * jnp.exp(stats[:, 0:1, :] - highest[None]), axis=0)
    return highest + jnp.log(total)


def flat_half(blocks):
    count, rows, width = blocks.shape
    return blocks.astype(jnp.float32).reshape(count * rows, width).astype(jnp.bfloat16)


def kernel(
    inner_count,
    line_count,
    pair_count,
    scale_ref,
    image_hbm,
    text_hbm,
    loss_ref,
    image_grad_ref,
    text_grad_ref,
    images,
    texts,
    row_stats,
    col_stats,
    row_sums,
    col_sums,
    image_parts,
    text_parts,
    image_slots,
    text_slots,
    image_own,
    text_own,
    image_ref,
    text_ref,
    input_sems,
    line_send,
    line_recv,
    plane_send,
    plane_recv,
):
    text_in = pltpu.make_async_copy(text_hbm, text_ref, input_sems.at[0])
    image_in = pltpu.make_async_copy(image_hbm, image_ref, input_sems.at[1])
    text_in.start()
    image_in.start()
    inner, blk = lax.axis_index("inner"), lax.axis_index("blk")
    place, side = blk // pair_count, lax.rem(blk, pair_count)
    line = Group(
        place, line_count, lambda z: (inner, z * pair_count + side), (line_send, line_recv)
    )
    plane = Group(
        inner * pair_count + side,
        inner_count * pair_count,
        lambda g: (g // pair_count, place * pair_count + lax.rem(g, pair_count)),
        (plane_send, plane_recv),
    )
    groups = (plane, line)
    barrier = pltpu.get_barrier_semaphore()
    for group in groups:
        for step in group.steps():
            pl.semaphore_signal(
                barrier, inc=1, device_id=group.device_of(group.on(step)), device_id_type=MESH
            )

    factor = scale_ref[0]
    text_in.wait()
    text_unit, text_inverse = unit_rows(text_ref[...])
    text_half = text_unit.astype(jnp.bfloat16)
    texts[plane.me] = text_half
    image_in.wait()
    image_unit, image_inverse = unit_rows(image_ref[...])
    image_half = image_unit.astype(jnp.bfloat16)
    images[line.me] = image_half
    pl.semaphore_wait(barrier, plane.size + line.size - 2)
    line.start_gather(images, 0)
    plane.start_gather(texts, 0)
    image_back = image_half.astype(jnp.float32)
    text_back = text_half.astype(jnp.float32)
    diagonal = factor * jnp.sum(image_back * text_back)
    plane.wait_gather(texts, 0)
    line.wait_gather(images, 0)

    image_group = flat_half(images[...])
    text_group = flat_half(texts[...])
    image_count, text_count = image_group.shape[0], text_group.shape[0]
    logits = factor * lax.dot_general(
        image_group, text_group, (((1,), (1,)), ((), ())), preferred_element_type=jnp.float32
    )
    row_peak = jnp.max(logits, axis=1, keepdims=True)
    row_total = jnp.sum(jnp.exp(logits - row_peak), axis=1, keepdims=True)
    col_peak = jnp.max(logits, axis=0, keepdims=True)
    col_total = jnp.sum(jnp.exp(logits - col_peak), axis=0, keepdims=True)
    row_stats[line.me, 0:1, :] = as_row(row_peak)
    row_stats[line.me, 1:2, :] = as_row(row_total)
    col_stats[plane.me, 0:1, :] = col_peak
    col_stats[plane.me, 1:2, :] = col_total
    col_stats[plane.me, 2:3, :] = jnp.full((1, text_count), diagonal, jnp.float32)
    line.start_gather(row_stats, 1)
    plane.start_gather(col_stats, 1)
    line.wait_gather(row_stats, 1)
    plane.wait_gather(col_stats, 1)
    row_lse = merge(row_stats[...])
    col_lse = merge(col_stats[...])

    tile = row_sums.shape[1:]
    plane_diagonal = jnp.sum(col_stats[:, 2, 0:1])
    row_sums[plane.me] = jnp.full(tile, jnp.sum(row_lse), jnp.float32)
    col_sums[line.me] = jnp.full(tile, jnp.sum(col_lse) - 2.0 * plane_diagonal, jnp.float32)
    plane.start_gather(row_sums, 3)
    line.start_gather(col_sums, 3)

    weights = (
        0.5 * factor * (jnp.exp(logits - as_column(row_lse)) + jnp.exp(logits - col_lse))
    ).astype(jnp.bfloat16)
    image_own[...] = jnp.dot(
        weights, text_group, preferred_element_type=jnp.float32
    ).reshape(image_parts.shape)
    image_parts[...] = image_own[...].astype(jnp.bfloat16)
    line.start_scatter(image_parts, image_slots, 2)
    text_own[...] = lax.dot_general(
        weights, image_group, (((0,), (0,)), ((), ())), preferred_element_type=jnp.float32
    ).reshape(text_parts.shape)
    text_parts[...] = text_own[...].astype(jnp.bfloat16)
    plane.start_scatter(text_parts, text_slots, 2)

    plane.wait_scatter(text_parts, text_slots, 2)
    text_sum = text_own[plane.me]
    for step in plane.steps():
        text_sum = text_sum + text_slots[step].astype(jnp.float32)
    text_grad_ref[...] = project(text_sum - factor * image_back, text_unit, text_inverse)
    line.wait_scatter(image_parts, image_slots, 2)
    image_sum = image_own[line.me]
    for step in line.steps():
        image_sum = image_sum + image_slots[step].astype(jnp.float32)
    image_grad_ref[...] = project(image_sum - factor * text_back, image_unit, image_inverse)

    plane.wait_gather(row_sums, 3)
    line.wait_gather(col_sums, 3)
    examples = 2.0 * line.size * plane.size * image_ref.shape[0]
    whole = jnp.sum(row_sums[...], axis=0)[0, 0] + jnp.sum(col_sums[...], axis=0)[0, 0]
    loss_ref[0] = whole / examples
    for buf_line, buf_plane, stage in (
        (images, texts, 0),
        (row_stats, col_stats, 1),
        (col_sums, row_sums, 3),
    ):
        line.end_gather(buf_line, stage)
        plane.end_gather(buf_plane, stage)


def solution(mesh):
    inner_count, blk_count = mesh.shape["inner"], mesh.shape["blk"]
    pair_count = 2 if blk_count % 2 == 0 else 1
    line_count = blk_count // pair_count
    plane_count = inner_count * pair_count

    def on_device(image_emb, text_emb, logit_scale):
        rows, width = image_emb.shape
        vmem = pl.BlockSpec(memory_space=pltpu.VMEM)
        hbm = pl.BlockSpec(memory_space=pl.ANY)
        smem = pl.BlockSpec(memory_space=pltpu.SMEM)
        near = pltpu.VMEM((rows, width), jnp.float32)
        return pl.pallas_call(
            functools.partial(kernel, inner_count, line_count, pair_count),
            out_shape=(jax.ShapeDtypeStruct((1,), jnp.float32), near, near),
            in_specs=[smem, hbm, hbm],
            out_specs=(smem, vmem, vmem),
            scratch_shapes=[
                pltpu.VMEM((line_count, rows, width), jnp.bfloat16),
                pltpu.VMEM((plane_count, rows, width), jnp.bfloat16),
                pltpu.VMEM((line_count, 2, line_count * rows), jnp.float32),
                pltpu.VMEM((plane_count, 4, plane_count * rows), jnp.float32),
                pltpu.VMEM((plane_count, 1, 128), jnp.float32),
                pltpu.VMEM((line_count, 1, 128), jnp.float32),
                pltpu.VMEM((line_count, rows, width), jnp.bfloat16),
                pltpu.VMEM((plane_count, rows, width), jnp.bfloat16),
                pltpu.VMEM((line_count, rows, width), jnp.bfloat16),
                pltpu.VMEM((plane_count, rows, width), jnp.bfloat16),
                pltpu.VMEM((line_count, rows, width), jnp.float32),
                pltpu.VMEM((plane_count, rows, width), jnp.float32),
                pltpu.VMEM((rows, width), jnp.float32),
                pltpu.VMEM((rows, width), jnp.float32),
                pltpu.SemaphoreType.DMA((2,)),
                pltpu.SemaphoreType.DMA((4, line_count)),
                pltpu.SemaphoreType.DMA((4, line_count)),
                pltpu.SemaphoreType.DMA((4, plane_count)),
                pltpu.SemaphoreType.DMA((4, plane_count)),
            ],
            compiler_params=pltpu.CompilerParams(
                collective_id=0, has_side_effects=True, vmem_limit_bytes=56 * 1024 * 1024
            ),
            name="contrastive",
        )(logit_scale, image_emb, text_emb)

    in_specs = (P(("inner", "blk"), None), P(("inner", "blk"), None), P())
    out_specs = (P(), P(("inner", "blk"), None), P(("inner", "blk"), None))
    return jax.shard_map(
        on_device, mesh=mesh, in_specs=in_specs, out_specs=out_specs, check_vma=False
    )
```

profile of v0, /device:TPU:0, one launch (start us, length us, event | category | flops | bytes accessed | tf_op | source)
XLA Modules:
  0.0 25.2 jit_solution(6924934027049376624)
XLA Ops:
  1.3 21.0 %contrastive.1 = (f32[1]{0:T(128)}, f32[24,768]{1,0:T(8,128)S(1)}, f32[24,768]{1,0:T(8,128)S(1)}) custom-call(f32[1]{0:T(128)S(6)} %copy.11.scale_ref, f32[24,768]{1,0:T(8,128)} %image_hbm.1, f32[24,768]{1,0:T(8,128)} %text_hbm.1), custom_call_target="tpu_custom_call" | custom-call | tf_op jit(solution)/shard_map/contrastive/pallas_call | solution.py:249
  22.3 0.6 %copy.9 = f32[24,768]{1,0:T(8,128)} copy(f32[24,768]{1,0:T(8,128)S(1)} %get-tuple-element.4) | data formatting | bytes 147456
  22.9 0.6 %copy.10 = f32[24,768]{1,0:T(8,128)} copy(f32[24,768]{1,0:T(8,128)S(1)} %get-tuple-element.5) | data formatting | bytes 147456
where the time goes:
time: 25.4 us; the launch traced here: 25.2 us
  Pallas kernels  21 us (83%)
  between operations  2.97 us (12%)
  local copies, waits for them, and re-layouts  1.27 us (5%)
    pallas_call x1, Pallas kernels, on_device(): pl.pallas_call(functools.partial(kernel, inner_count, line_count, pair_co...  21 us
    unnamed x2, local copies, waits for them, and re-layouts  1.27 us

commit v1 on v0

--- a/solution.py
+++ b/solution.py
@@ -21,53 +21,58 @@
 
 
 class Group:
-    def __init__(self, me, size, device_of, sems):
+    def __init__(self, me, size, device_of, order, sems):
         self.me, self.size, self.device_of, self.sems = me, size, device_of, sems
-
-    def on(self, step):
-        return lax.rem(self.me + step, self.size)
-
-    def back(self, step):
-        return lax.rem(self.me + self.size - step, self.size)
-
-    def copy(self, src, dst, stage, step, to):
+        self.order = order
+
+    def others(self, reverse=False):
+        steps = range(1, self.size)
+        return [self.order(self.me, self.size, k) for k in (reversed(steps) if reverse else steps)]
+
+    def copy(self, src, dst, stage, to):
         send_sems, recv_sems = self.sems
         return pltpu.make_async_remote_copy(
             src_ref=src,
             dst_ref=dst,
-            send_sem=send_sems.at[stage, step],
-            recv_sem=recv_sems.at[stage, step],
+            send_sem=send_sems.at[stage],
+            recv_sem=recv_sems.at[stage],
             device_id=self.device_of(to),
             device_id_type=MESH,
         )
 
-    def steps(self):
-        return range(1, self.size)
-
-    def start_gather(self, buf, stage):
+    def whole(self, buf, stage):
+        part = buf.at[pl.ds(0, self.size - 1)]
+        return self.copy(part, part, stage, self.order(self.me, self.size, 1))
+
+    def start_gather(self, buf, stage, reverse=False):
         mine = buf.at[self.me]
-        for step in self.steps():
-            self.copy(mine, mine, stage, step, self.on(step)).start()
-
-    def wait_gather(self, buf, stage):
-        for step in self.steps():
-            theirs = buf.at[self.back(step)]
-            self.copy(theirs, theirs, stage, step, self.back(step)).wait_recv()
-
-    def end_gather(self, buf, stage):
-        mine = buf.at[self.me]
-        for step in self.steps():
-            self.copy(mine, mine, stage, step, self.on(step)).wait_send()
-
-    def start_scatter(self, parts, slots, stage):
-        for step in self.steps():
-            to = self.on(step)
-            self.copy(parts.at[to], slots.at[step], stage, step, to).start()
-
-    def wait_scatter(self, parts, slots, stage):
-        for step in self.steps():
-            to = self.on(step)
-            self.copy(parts.at[to], slots.at[step], stage, step, to).wait()
+        for to in self.others(reverse):
+            self.copy(mine, mine, stage, to).start()
+
+    def wait_recv(self, buf, stage):
+        self.whole(buf, stage).wait_recv()
+
+    def wait_send(self, buf, stage):
+        self.whole(buf, stage).wait_send()
+
+    def start_scatter(self, parts, slots, stage, reverse=False):
+        for to in self.others(reverse):
+            self.copy(parts.at[to], slots.at[self.me], stage, to).start()
+
+
+def ascending(me, size, k):
+    return k - 1 + (k - 1 >= me).astype(jnp.int32)
+
+
+def flipped(me, size, k):
+    if size & (size - 1):
+        return lax.rem(me + k, size)
+    out, bit = me, 1
+    while bit <= k:
+        if k & bit:
+            out = out + bit * (1 - 2 * lax.rem(me // bit, 2))
+        bit *= 2
+    return out
 
 
 def as_column(row):
@@ -102,9 +107,7 @@
     scale_ref,
     image_hbm,
     text_hbm,
-    loss_ref,
-    image_grad_ref,
-    text_grad_ref,
+    packed_ref,
     images,
     texts,
     row_stats,
@@ -132,20 +135,25 @@
     inner, blk = lax.axis_index("inner"), lax.axis_index("blk")
     place, side = blk // pair_count, lax.rem(blk, pair_count)
     line = Group(
-        place, line_count, lambda z: (inner, z * pair_count + side), (line_send, line_recv)
+        place,
+        line_count,
+        lambda z: (inner, z * pair_count + side),
+        ascending,
+        (line_send, line_recv),
     )
     plane = Group(
         inner * pair_count + side,
         inner_count * pair_count,
         lambda g: (g // pair_count, place * pair_count + lax.rem(g, pair_count)),
+        flipped,
         (plane_send, plane_recv),
     )
     groups = (plane, line)
     barrier = pltpu.get_barrier_semaphore()
     for group in groups:
-        for step in group.steps():
+        for to in group.others():
             pl.semaphore_signal(
-                barrier, inc=1, device_id=group.device_of(group.on(step)), device_id_type=MESH
+                barrier, inc=1, device_id=group.device_of(to), device_id_type=MESH
             )
 
     factor = scale_ref[0]
@@ -158,13 +166,13 @@
     image_half = image_unit.astype(jnp.bfloat16)
     images[line.me] = image_half
     pl.semaphore_wait(barrier, plane.size + line.size - 2)
-    line.start_gather(images, 0)
-    plane.start_gather(texts, 0)
+    line.start_gather(images, 0, reverse=True)
+    plane.start_gather(texts, 0, reverse=True)
     image_back = image_half.astype(jnp.float32)
     text_back = text_half.astype(jnp.float32)
     diagonal = factor * jnp.sum(image_back * text_back)
-    plane.wait_gather(texts, 0)
-    line.wait_gather(images, 0)
+    plane.wait_recv(texts, 0)
+    line.wait_recv(images, 0)
 
     image_group = flat_half(images[...])
     text_group = flat_half(texts[...])
@@ -182,9 +190,9 @@
     col_stats[plane.me, 1:2, :] = col_total
     col_stats[plane.me, 2:3, :] = jnp.full((1, text_count), diagonal, jnp.float32)
     line.start_gather(row_stats, 1)
-    plane.start_gather(col_stats, 1)
-    line.wait_gather(row_stats, 1)
-    plane.wait_gather(col_stats, 1)
+    plane.start_gather(col_stats, 1, reverse=True)
+    line.wait_recv(row_stats, 1)
+    plane.wait_recv(col_stats, 1)
     row_lse = merge(row_stats[...])
     col_lse = merge(col_stats[...])
 
@@ -209,29 +217,31 @@
     text_parts[...] = text_own[...].astype(jnp.bfloat16)
     plane.start_scatter(text_parts, text_slots, 2)
 
-    plane.wait_scatter(text_parts, text_slots, 2)
+    rows = image_ref.shape[0]
+    plane.wait_recv(text_slots, 2)
     text_sum = text_own[plane.me]
-    for step in plane.steps():
-        text_sum = text_sum + text_slots[step].astype(jnp.float32)
-    text_grad_ref[...] = project(text_sum - factor * image_back, text_unit, text_inverse)
-    line.wait_scatter(image_parts, image_slots, 2)
+    for other in plane.others():
+        text_sum = text_sum + text_slots[other].astype(jnp.float32)
+    packed_ref[pl.ds(rows, rows)] = project(text_sum - factor * image_back, text_unit, text_inverse)
+    line.wait_recv(image_slots, 2)
     image_sum = image_own[line.me]
-    for step in line.steps():
-        image_sum = image_sum + image_slots[step].astype(jnp.float32)
-    image_grad_ref[...] = project(image_sum - factor * text_back, image_unit, image_inverse)
-
-    plane.wait_gather(row_sums, 3)
-    line.wait_gather(col_sums, 3)
-    examples = 2.0 * line.size * plane.size * image_ref.shape[0]
-    whole = jnp.sum(row_sums[...], axis=0)[0, 0] + jnp.sum(col_sums[...], axis=0)[0, 0]
-    loss_ref[0] = whole / examples
+    for other in line.others():
+        image_sum = image_sum + image_slots[other].astype(jnp.float32)
+    packed_ref[pl.ds(0, rows)] = project(image_sum - factor * text_back, image_unit, image_inverse)
+
+    plane.wait_recv(row_sums, 3)
+    line.wait_recv(col_sums, 3)
+    examples = 2.0 * line.size * plane.size * rows
+    whole = jnp.sum(row_sums[...], axis=0)[0:1, 0:1] + jnp.sum(col_sums[...], axis=0)[0:1, 0:1]
+    packed_ref[pl.ds(2 * rows, 8)] = jnp.broadcast_to(whole / examples, (8, packed_ref.shape[1]))
     for buf_line, buf_plane, stage in (
         (images, texts, 0),
         (row_stats, col_stats, 1),
+        (image_parts, text_parts, 2),
         (col_sums, row_sums, 3),
     ):
-        line.end_gather(buf_line, stage)
-        plane.end_gather(buf_plane, stage)
+        line.wait_send(buf_line, stage)
+        plane.wait_send(buf_plane, stage)
 
 
 def solution(mesh):
@@ -245,12 +255,11 @@
         vmem = pl.BlockSpec(memory_space=pltpu.VMEM)
         hbm = pl.BlockSpec(memory_space=pl.ANY)
         smem = pl.BlockSpec(memory_space=pltpu.SMEM)
-        near = pltpu.VMEM((rows, width), jnp.float32)
-        return pl.pallas_call(
+        packed = pl.pallas_call(
             functools.partial(kernel, inner_count, line_count, pair_count),
-            out_shape=(jax.ShapeDtypeStruct((1,), jnp.float32), near, near),
+            out_shape=pltpu.VMEM((2 * rows + 8, width), jnp.float32),
             in_specs=[smem, hbm, hbm],
-            out_specs=(smem, vmem, vmem),
+            out_specs=vmem,
             scratch_shapes=[
                 pltpu.VMEM((line_count, rows, width), jnp.bfloat16),
                 pltpu.VMEM((plane_count, rows, width), jnp.bfloat16),
@@ -267,16 +276,17 @@
                 pltpu.VMEM((rows, width), jnp.float32),
                 pltpu.VMEM((rows, width), jnp.float32),
                 pltpu.SemaphoreType.DMA((2,)),
-                pltpu.SemaphoreType.DMA((4, line_count)),
-                pltpu.SemaphoreType.DMA((4, line_count)),
-                pltpu.SemaphoreType.DMA((4, plane_count)),
-                pltpu.SemaphoreType.DMA((4, plane_count)),
+                pltpu.SemaphoreType.DMA((4,)),
+                pltpu.SemaphoreType.DMA((4,)),
+                pltpu.SemaphoreType.DMA((4,)),
+                pltpu.SemaphoreType.DMA((4,)),
             ],
             compiler_params=pltpu.CompilerParams(
                 collective_id=0, has_side_effects=True, vmem_limit_bytes=56 * 1024 * 1024
             ),
             name="contrastive",
         )(logit_scale, image_emb, text_emb)
+        return packed[2 * rows, 0:1], packed[0:rows], packed[rows : 2 * rows]
 
     in_specs = (P(("inner", "blk"), None), P(("inner", "blk"), None), P())
     out_specs = (P(), P(("inner", "blk"), None), P(("inner", "blk"), None))

time: 25.4 us -> 23.1 us (0.909)
  between operations: 2.97 us -> 1.29 us
  Pallas kernels: 21 us -> 20.5 us
    unnamed x2 -> x0, local copies, waits for them, and re-layouts: 1.27 us -> none
    slice x0 -> x2, local copies, waits for them, and re-layouts: none -> 1.18 us  [on_device(): return (packed[2 * rows, 0:1], packed[0:rows], packed[rows:2 * rows])]
    pallas_call x1, Pallas kernels: 21 us -> 20.5 us  [on_device(): pl.pallas_call(functools.partial(kernel, inner_count, line_count, pair_co...]
where the time goes in v1:
time: 23.1 us; the launch traced here: 23 us
  Pallas kernels  20.5 us (89%)
  between operations  1.29 us (6%)
  local copies, waits for them, and re-layouts  1.18 us (5%)
    pallas_call x1, Pallas kernels, on_device(): pl.pallas_call(functools.partial(kernel, inner_count, line_count, pair_co...  20.5 us
    slice x2, local copies, waits for them, and re-layouts, on_device(): return (packed[2 * rows, 0:1], packed[0:rows], packed[rows:2 * rows])  1.18 us

profile of v1, /device:TPU:0, one launch (start us, length us, event | category | flops | bytes accessed | tf_op | source)
XLA Modules:
  0.0 23.0 jit_solution(8942837974372222554)
XLA Ops:
  1.3 20.5 %contrastive.1 = f32[56,768]{1,0:T(8,128)S(1)} custom-call(f32[1]{0:T(128)S(6)} %copy.6.scale_ref, f32[24,768]{1,0:T(8,128)} %image_hbm.1, f32[24,768]{1,0:T(8,128)} %text_hbm.1), custom_call_target="tpu_custom_call" | custom-call | tf_op jit(solution)/shard_map/contrastive/pallas_call | solution.py:258
  21.8 0.7 %fusion = (f32[24,768]{1,0:T(8,128)}, f32[24,768]{1,0:T(8,128)}) fusion(f32[56,768]{1,0:T(8,128)S(1)} %contrastive.1), kind=kLoop, calls=%fused_computation | loop fusion | bytes 294912 | tf_op jit(solution)/shard_map/slice | solution.py:289
  22.4 0.5 %slice.9 = f32[1,1]{1,0:T(1,128)} slice(f32[56,768]{1,0:T(8,128)S(1)} %contrastive.1), slice={[48:49], [0:1]} | slice | bytes 8 | tf_op jit(solution)/shard_map/slice | solution.py:289

commit v2 on v1

--- a/solution.py
+++ b/solution.py
@@ -25,9 +25,9 @@
         self.me, self.size, self.device_of, self.sems = me, size, device_of, sems
         self.order = order
 
-    def others(self, reverse=False):
-        steps = range(1, self.size)
-        return [self.order(self.me, self.size, k) for k in (reversed(steps) if reverse else steps)]
+    def others(self, order=None):
+        order = order or self.order
+        return [order(self.me, self.size, k) for k in range(1, self.size)]
 
     def copy(self, src, dst, stage, to):
         send_sems, recv_sems = self.sems
@@ -44,9 +44,9 @@
         part = buf.at[pl.ds(0, self.size - 1)]
         return self.copy(part, part, stage, self.order(self.me, self.size, 1))
 
-    def start_gather(self, buf, stage, reverse=False):
+    def start_gather(self, buf, stage, order=None):
         mine = buf.at[self.me]
-        for to in self.others(reverse):
+        for to in self.others(order):
             self.copy(mine, mine, stage, to).start()
 
     def wait_recv(self, buf, stage):
@@ -55,8 +55,8 @@
     def wait_send(self, buf, stage):
         self.whole(buf, stage).wait_send()
 
-    def start_scatter(self, parts, slots, stage, reverse=False):
-        for to in self.others(reverse):
+    def start_scatter(self, parts, slots, stage, order=None):
+        for to in self.others(order):
             self.copy(parts.at[to], slots.at[self.me], stage, to).start()
 
 
@@ -64,7 +64,12 @@
     return k - 1 + (k - 1 >= me).astype(jnp.int32)
 
 
-def flipped(me, size, k):
+def far_first(me, size, k):
+    low = size - k - (size - k <= me).astype(jnp.int32)
+    return jnp.where(2 * me < size, low, ascending(me, size, k))
+
+
+def turned(me, size, k):
     if size & (size - 1):
         return lax.rem(me + k, size)
     out, bit = me, 1
@@ -73,6 +78,10 @@
             out = out + bit * (1 - 2 * lax.rem(me // bit, 2))
         bit *= 2
     return out
+
+
+def flipped(me, size, k):
+    return turned(me, size, size - k)
 
 
 def as_column(row):
@@ -127,6 +136,7 @@
     line_recv,
     plane_send,
     plane_recv,
+    ready,
 ):
     text_in = pltpu.make_async_copy(text_hbm, text_ref, input_sems.at[0])
     image_in = pltpu.make_async_copy(image_hbm, image_ref, input_sems.at[1])
@@ -148,13 +158,16 @@
         flipped,
         (plane_send, plane_recv),
     )
-    groups = (plane, line)
     barrier = pltpu.get_barrier_semaphore()
-    for group in groups:
-        for to in group.others():
-            pl.semaphore_signal(
-                barrier, inc=1, device_id=group.device_of(to), device_id_type=MESH
-            )
+    pair = lambda c: (inner, place * pair_count + c)
+    meets = [pair(c) for c in [lax.rem(side + k, pair_count) for k in range(1, pair_count)]]
+    meets += [(inner, z * pair_count) for z in line.others()]
+    meets += [
+        (g, place * pair_count + pair_count - 1)
+        for g in [ascending(inner, inner_count, k) for k in range(1, inner_count)]
+    ]
+    for to in meets:
+        pl.semaphore_signal(barrier, inc=1, device_id=to, device_id_type=MESH)
 
     factor = scale_ref[0]
     text_in.wait()
@@ -165,14 +178,63 @@
     image_unit, image_inverse = unit_rows(image_ref[...])
     image_half = image_unit.astype(jnp.bfloat16)
     images[line.me] = image_half
-    pl.semaphore_wait(barrier, plane.size + line.size - 2)
-    line.start_gather(images, 0, reverse=True)
-    plane.start_gather(texts, 0, reverse=True)
+    chips = range(1, inner_count)
+    near = [k for k in chips if k & (k - 1) == 0] if pair_count == 2 else list(chips)
+    far = [k for k in chips if k not in near]
+    chip_at = lambda k: turned(inner, inner_count, k)
+    slot = lambda g, c: texts.at[g * pair_count + c]
+
+    def text_copy(block, g, c, stage):
+        return plane.copy(block, block, stage, g * pair_count + c)
+
+    def start_texts():
+        mine = slot(inner, side)
+        for k in reversed(far):
+            text_copy(mine, chip_at(k), side, 4).start()
+        for k in near:
+            for c in range(pair_count):
+                text_copy(mine, chip_at(k), c, 0).start()
+        if pair_count == 2:
+            text_copy(mine, inner, 1 - side, 0).start()
+
+    def some(count, stage):
+        blocks = texts.at[pl.ds(0, count)]
+        return plane.copy(blocks, blocks, stage, inner * pair_count + 1 - side)
+
+    near_blocks = pair_count * len(near) + pair_count - 1
+
+    line_met, plane_met = pair_count * (line_count - 1), pair_count * (inner_count - 1)
+    if pair_count == 1:
+        pl.semaphore_wait(barrier, line_met + plane_met)
+        line.start_gather(images, 0, far_first)
+        start_texts()
+    else:
+        pl.semaphore_wait(barrier, 1 + line_met + side * (plane_met - line_met))
+        pl.semaphore_signal(ready, inc=1, device_id=pair(1 - side), device_id_type=MESH)
+
+        @pl.when(side == 0)
+        def _():
+            line.start_gather(images, 0, far_first)
+            pl.semaphore_wait(ready, 1)
+            start_texts()
+
+        @pl.when(side == 1)
+        def _():
+            start_texts()
+            pl.semaphore_wait(ready, 1)
+            line.start_gather(images, 0, far_first)
+
     image_back = image_half.astype(jnp.float32)
     text_back = text_half.astype(jnp.float32)
     diagonal = factor * jnp.sum(image_back * text_back)
-    plane.wait_recv(texts, 0)
+    if far:
+        some(len(far), 4).wait_recv()
+        for k in far:
+            text_copy(slot(chip_at(k), side), inner, 1 - side, 5).start()
+    some(near_blocks, 0).wait_recv()
     line.wait_recv(images, 0)
+    if far:
+        some(len(far), 5).wait_recv()
 
     image_group = flat_half(images[...])
     text_group = flat_half(texts[...])
@@ -190,7 +252,7 @@
     col_stats[plane.me, 1:2, :] = col_total
     col_stats[plane.me, 2:3, :] = jnp.full((1, text_count), diagonal, jnp.float32)
     line.start_gather(row_stats, 1)
-    plane.start_gather(col_stats, 1, reverse=True)
+    plane.start_gather(col_stats, 1)
     line.wait_recv(row_stats, 1)
     plane.wait_recv(col_stats, 1)
     row_lse = merge(row_stats[...])
@@ -215,7 +277,7 @@
         weights, image_group, (((0,), (0,)), ((), ())), preferred_element_type=jnp.float32
     ).reshape(text_parts.shape)
     text_parts[...] = text_own[...].astype(jnp.bfloat16)
-    plane.start_scatter(text_parts, text_slots, 2)
+    plane.start_scatter(text_parts, text_slots, 2, ascending)
 
     rows = image_ref.shape[0]
     plane.wait_recv(text_slots, 2)
@@ -234,8 +296,12 @@
     examples = 2.0 * line.size * plane.size * rows
     whole = jnp.sum(row_sums[...], axis=0)[0:1, 0:1] + jnp.sum(col_sums[...], axis=0)[0:1, 0:1]
     packed_ref[pl.ds(2 * rows, 8)] = jnp.broadcast_to(whole / examples, (8, packed_ref.shape[1]))
+    line.wait_send(images, 0)
+    some(near_blocks, 0).wait_send()
+    if far:
+        some(len(far), 4).wait_send()
+        some(len(far), 5).wait_send()
     for buf_line, buf_plane, stage in (
-        (images, texts, 0),
         (row_stats, col_stats, 1),
         (image_parts, text_parts, 2),
         (col_sums, row_sums, 3),
@@ -278,8 +344,9 @@
                 pltpu.SemaphoreType.DMA((2,)),
                 pltpu.SemaphoreType.DMA((4,)),
                 pltpu.SemaphoreType.DMA((4,)),
-                pltpu.SemaphoreType.DMA((4,)),
-                pltpu.SemaphoreType.DMA((4,)),
+                pltpu.SemaphoreType.DMA((6,)),
+                pltpu.SemaphoreType.DMA((6,)),
+                pltpu.SemaphoreType.REGULAR,
             ],
             compiler_params=pltpu.CompilerParams(
                 collective_id=0, has_side_effects=True, vmem_limit_bytes=56 * 1024 * 1024

time: 23.1 us -> 22.6 us (0.978)
  Pallas kernels: 20.5 us -> 19.9 us
    pallas_call x1, Pallas kernels: 20.5 us -> 19.9 us  [on_device(): pl.pallas_call(functools.partial(kernel, inner_count, line_count, pair_co...]
where the time goes in v2:
time: 22.6 us; the launch traced here: 22.4 us
  Pallas kernels  19.9 us (88%)
  between operations  1.29 us (6%)
  local copies, waits for them, and re-layouts  1.18 us (5%)
    pallas_call x1, Pallas kernels, on_device(): pl.pallas_call(functools.partial(kernel, inner_count, line_count, pair_co...  19.9 us
    slice x2, local copies, waits for them, and re-layouts, on_device(): return (packed[2 * rows, 0:1], packed[0:rows], packed[rows:2 * rows])  1.18 us

profile of v2, /device:TPU:0, one launch (start us, length us, event | category | flops | bytes accessed | tf_op | source)
XLA Modules:
  0.0 22.4 jit_solution(12372434568887868626)
XLA Ops:
  1.3 19.9 %contrastive.1 = f32[56,768]{1,0:T(8,128)S(1)} custom-call(f32[1]{0:T(128)S(6)} %copy.6.scale_ref, f32[24,768]{1,0:T(8,128)} %image_hbm.1, f32[24,768]{1,0:T(8,128)} %text_hbm.1), custom_call_target="tpu_custom_call" | custom-call | tf_op jit(solution)/shard_map/contrastive/pallas_call | solution.py:324
  21.2 0.7 %fusion = (f32[24,768]{1,0:T(8,128)}, f32[24,768]{1,0:T(8,128)}) fusion(f32[56,768]{1,0:T(8,128)S(1)} %contrastive.1), kind=kLoop, calls=%fused_computation | loop fusion | bytes 294912 | tf_op jit(solution)/shard_map/slice | solution.py:356
  21.9 0.5 %slice.9 = f32[1,1]{1,0:T(1,128)} slice(f32[56,768]{1,0:T(8,128)S(1)} %contrastive.1), slice={[48:49], [0:1]} | slice | bytes 8 | tf_op jit(solution)/shard_map/slice | solution.py:356

commit v3 on v2

--- a/solution.py
+++ b/solution.py
@@ -55,8 +55,8 @@
     def wait_send(self, buf, stage):
         self.whole(buf, stage).wait_send()
 
-    def start_scatter(self, parts, slots, stage, order=None):
-        for to in self.others(order):
+    def start_scatter(self, parts, slots, stage, order=None, part=slice(None)):
+        for to in self.others(order)[part]:
             self.copy(parts.at[to], slots.at[self.me], stage, to).start()
 
 
@@ -116,7 +116,9 @@
     scale_ref,
     image_hbm,
     text_hbm,
-    packed_ref,
+    loss_ref,
+    image_grad_ref,
+    text_grad_ref,
     images,
     texts,
     row_stats,
@@ -258,13 +260,6 @@
     row_lse = merge(row_stats[...])
     col_lse = merge(col_stats[...])
 
-    tile = row_sums.shape[1:]
-    plane_diagonal = jnp.sum(col_stats[:, 2, 0:1])
-    row_sums[plane.me] = jnp.full(tile, jnp.sum(row_lse), jnp.float32)
-    col_sums[line.me] = jnp.full(tile, jnp.sum(col_lse) - 2.0 * plane_diagonal, jnp.float32)
-    plane.start_gather(row_sums, 3)
-    line.start_gather(col_sums, 3)
-
     weights = (
         0.5 * factor * (jnp.exp(logits - as_column(row_lse)) + jnp.exp(logits - col_lse))
     ).astype(jnp.bfloat16)
@@ -272,30 +267,38 @@
         weights, text_group, preferred_element_type=jnp.float32
     ).reshape(image_parts.shape)
     image_parts[...] = image_own[...].astype(jnp.bfloat16)
-    line.start_scatter(image_parts, image_slots, 2)
+    line.start_scatter(image_parts, image_slots, 2, part=slice(0, 1))
     text_own[...] = lax.dot_general(
         weights, image_group, (((0,), (0,)), ((), ())), preferred_element_type=jnp.float32
     ).reshape(text_parts.shape)
     text_parts[...] = text_own[...].astype(jnp.bfloat16)
-    plane.start_scatter(text_parts, text_slots, 2, ascending)
+    plane.start_scatter(text_parts, text_slots, 2, ascending, slice(0, pair_count))
+    tile = row_sums.shape[1:]
+    plane_diagonal = jnp.sum(col_stats[:, 2, 0:1])
+    row_sums[plane.me] = jnp.full(tile, jnp.sum(row_lse), jnp.float32)
+    col_sums[line.me] = jnp.full(tile, jnp.sum(col_lse) - 2.0 * plane_diagonal, jnp.float32)
+    plane.start_gather(row_sums, 3)
+    line.start_gather(col_sums, 3)
+    line.start_scatter(image_parts, image_slots, 2, part=slice(1, None))
+    plane.start_scatter(text_parts, text_slots, 2, ascending, slice(pair_count, None))
 
     rows = image_ref.shape[0]
     plane.wait_recv(text_slots, 2)
     text_sum = text_own[plane.me]
     for other in plane.others():
         text_sum = text_sum + text_slots[other].astype(jnp.float32)
-    packed_ref[pl.ds(rows, rows)] = project(text_sum - factor * image_back, text_unit, text_inverse)
+    text_grad_ref[...] = project(text_sum - factor * image_back, text_unit, text_inverse)
     line.wait_recv(image_slots, 2)
     image_sum = image_own[line.me]
     for other in line.others():
         image_sum = image_sum + image_slots[other].astype(jnp.float32)
-    packed_ref[pl.ds(0, rows)] = project(image_sum - factor * text_back, image_unit, image_inverse)
+    image_grad_ref[...] = project(image_sum - factor * text_back, image_unit, image_inverse)
 
     plane.wait_recv(row_sums, 3)
     line.wait_recv(col_sums, 3)
     examples = 2.0 * line.size * plane.size * rows
     whole = jnp.sum(row_sums[...], axis=0)[0:1, 0:1] + jnp.sum(col_sums[...], axis=0)[0:1, 0:1]
-    packed_ref[pl.ds(2 * rows, 8)] = jnp.broadcast_to(whole / examples, (8, packed_ref.shape[1]))
+    loss_ref[...] = jnp.broadcast_to(whole / examples, loss_ref.shape)
     line.wait_send(images, 0)
     some(near_blocks, 0).wait_send()
     if far:
@@ -310,6 +313,15 @@
         plane.wait_send(buf_plane, stage)
 
 
+def store(loss, image_grad, text_grad, loss_hbm, image_hbm, text_hbm, sems):
+    pairs = ((image_grad, image_hbm), (text_grad, text_hbm), (loss, loss_hbm))
+    copies = [pltpu.make_async_copy(*pair, sems.at[k]) for k, pair in enumerate(pairs)]
+    for copy in copies:
+        copy.start()
+    for copy in copies:
+        copy.wait()
+
+
 def solution(mesh):
     inner_count, blk_count = mesh.shape["inner"], mesh.shape["blk"]
     pair_count = 2 if blk_count % 2 == 0 else 1
@@ -321,11 +333,12 @@
         vmem = pl.BlockSpec(memory_space=pltpu.VMEM)
         hbm = pl.BlockSpec(memory_space=pl.ANY)
         smem = pl.BlockSpec(memory_space=pltpu.SMEM)
-        packed = pl.pallas_call(
+        near = pltpu.VMEM((rows, width), jnp.float32)
+        results = pl.pallas_call(
             functools.partial(kernel, inner_count, line_count, pair_count),
-            out_shape=pltpu.VMEM((2 * rows + 8, width), jnp.float32),
+            out_shape=(pltpu.VMEM((1, 128), jnp.float32), near, near),
             in_specs=[smem, hbm, hbm],
-            out_specs=vmem,
+            out_specs=(vmem, vmem, vmem),
             scratch_shapes=[
                 pltpu.VMEM((line_count, rows, width), jnp.bfloat16),
                 pltpu.VMEM((plane_count, rows, width), jnp.bfloat16),
@@ -353,7 +366,17 @@
             ),
             name="contrastive",
         )(logit_scale, image_emb, text_emb)
-        return packed[2 * rows, 0:1], packed[0:rows], packed[rows : 2 * rows]
+        far = jax.ShapeDtypeStruct((rows, width), jnp.float32)
+        loss, image_grad, text_grad = pl.pallas_call(
+            store,
+            out_shape=(jax.ShapeDtypeStruct((1, 128), jnp.float32), far, far),
+            in_specs=[vmem, vmem, vmem],
+            out_specs=(hbm, hbm, hbm),
+            scratch_shapes=[pltpu.SemaphoreType.DMA((3,))],
+            compiler_params=pltpu.CompilerParams(vmem_limit_bytes=16 * 1024 * 1024),
+            name="store",
+        )(*results)
+        return loss.reshape(128)[0:1], image_grad, text_grad
 
     in_specs = (P(("inner", "blk"), None), P(("inner", "blk"), None), P())
     out_specs = (P(), P(("inner", "blk"), None), P(("inner", "blk"), None))

time: 22.6 us -> 22.1 us (0.978)
  local copies, waits for them, and re-layouts: 1.18 us -> 0 us
  Pallas kernels: 19.9 us -> 20.6 us
    slice x2 -> x0, local copies, waits for them, and re-layouts: 1.18 us -> none  [on_device(): return (packed[2 * rows, 0:1], packed[0:rows], packed[rows:2 * rows])]
    pallas_call x0 -> x1, Pallas kernels: none -> 0.69 us  [on_device(): pl.pallas_call(store, out_shape=(jax.ShapeDtypeStruct((1, 128), jnp.float...]
where the time goes in v3:
time: 22.1 us; the launch traced here: 21.9 us
  Pallas kernels  20.6 us (93%)
  between operations  1.28 us (6%)
    pallas_call x1, Pallas kernels, on_device(): pl.pallas_call(functools.partial(kernel, inner_count, line_count, pair_co...  19.9 us
    pallas_call x1, Pallas kernels, on_device(): pl.pallas_call(store, out_shape=(jax.ShapeDtypeStruct((1, 128), jnp.float...  0.69 us

profile of v3, /device:TPU:0, one launch (start us, length us, event | category | flops | bytes accessed | tf_op | source)
XLA Modules:
  0.0 21.9 jit_solution(2498157453811724382)
XLA Ops:
  1.3 19.9 %contrastive.1 = (f32[1,128]{1,0:T(1,128)S(1)}, f32[24,768]{1,0:T(8,128)S(1)}, f32[24,768]{1,0:T(8,128)S(1)}) custom-call(f32[1]{0:T(128)S(6)} %copy.6.scale_ref, f32[24,768]{1,0:T(8,128)} %image_hbm.1, f32[24,768]{1,0:T(8,128)} %text_hbm.1), custom_call_target="tpu_custom_call" | custom-call | tf_op jit(solution)/shard_map/contrastive/pallas_call | solution.py:337
  21.2 0.7 %store.1 = (f32[1,128]{1,0:T(1,128)}, f32[24,768]{1,0:T(8,128)}, f32[24,768]{1,0:T(8,128)}) custom-call(f32[1,128]{1,0:T(1,128)S(1)} %get-tuple-element.9.loss, f32[24,768]{1,0:T(8,128)S(1)} %get-tuple-element.10.image_grad, f32[24,768]{1,0:T(8,128)S(1)} %get-tuple-element.11.text_grad), custom_call_target="tpu_custom_call" | custom-call | tf_op jit(solution)/shard_map/store/pallas_call | solution.py:370

commit v4 on v3

--- a/solution.py
+++ b/solution.py
@@ -29,12 +29,12 @@
         order = order or self.order
         return [order(self.me, self.size, k) for k in range(1, self.size)]
 
-    def copy(self, src, dst, stage, to):
+    def copy(self, src, dst, stage, to, later=None):
         send_sems, recv_sems = self.sems
         return pltpu.make_async_remote_copy(
             src_ref=src,
             dst_ref=dst,
-            send_sem=send_sems.at[stage],
+            send_sem=send_sems.at[stage if later is None else later],
             recv_sem=recv_sems.at[stage],
             device_id=self.device_of(to),
             device_id_type=MESH,
@@ -55,9 +55,13 @@
     def wait_send(self, buf, stage):
         self.whole(buf, stage).wait_send()
 
-    def start_scatter(self, parts, slots, stage, order=None, part=slice(None)):
+    def wait_some(self, buf, stage, count):
+        part = buf.at[pl.ds(0, count)]
+        self.copy(part, part, stage, self.order(self.me, self.size, 1)).wait_send()
+
+    def start_scatter(self, parts, slots, stage, order=None, part=slice(None), later=None):
         for to in self.others(order)[part]:
-            self.copy(parts.at[to], slots.at[self.me], stage, to).start()
+            self.copy(parts.at[to], slots.at[self.me], stage, to, later).start()
 
 
 def ascending(me, size, k):
@@ -138,7 +142,6 @@
     line_recv,
     plane_send,
     plane_recv,
-    ready,
 ):
     text_in = pltpu.make_async_copy(text_hbm, text_ref, input_sems.at[0])
     image_in = pltpu.make_async_copy(image_hbm, image_ref, input_sems.at[1])
@@ -161,13 +164,7 @@
         (plane_send, plane_recv),
     )
     barrier = pltpu.get_barrier_semaphore()
-    pair = lambda c: (inner, place * pair_count + c)
-    meets = [pair(c) for c in [lax.rem(side + k, pair_count) for k in range(1, pair_count)]]
-    meets += [(inner, z * pair_count) for z in line.others()]
-    meets += [
-        (g, place * pair_count + pair_count - 1)
-        for g in [ascending(inner, inner_count, k) for k in range(1, inner_count)]
-    ]
+    meets = [group.device_of(to) for group in (plane, line) for to in group.others()]
     for to in meets:
         pl.semaphore_signal(barrier, inc=1, device_id=to, device_id_type=MESH)
 
@@ -205,27 +202,9 @@
 
     near_blocks = pair_count * len(near) + pair_count - 1
 
-    line_met, plane_met = pair_count * (line_count - 1), pair_count * (inner_count - 1)
-    if pair_count == 1:
-        pl.semaphore_wait(barrier, line_met + plane_met)
-        line.start_gather(images, 0, far_first)
-        start_texts()
-    else:
-        pl.semaphore_wait(barrier, 1 + line_met + side * (plane_met - line_met))
-        pl.semaphore_signal(ready, inc=1, device_id=pair(1 - side), device_id_type=MESH)
-
-        @pl.when(side == 0)
-        def _():
-            line.start_gather(images, 0, far_first)
-            pl.semaphore_wait(ready, 1)
-            start_texts()
-
-        @pl.when(side == 1)
-        def _():
-            start_texts()
-            pl.semaphore_wait(ready, 1)
-            line.start_gather(images, 0, far_first)
-
+    pl.semaphore_wait(barrier, plane.size + line.size - 2)
+    line.start_gather(images, 0, far_first)
+    start_texts()
     image_back = image_half.astype(jnp.float32)
     text_back = text_half.astype(jnp.float32)
     diagonal = factor * jnp.sum(image_back * text_back)
@@ -279,8 +258,9 @@
     col_sums[line.me] = jnp.full(tile, jnp.sum(col_lse) - 2.0 * plane_diagonal, jnp.float32)
     plane.start_gather(row_sums, 3)
     line.start_gather(col_sums, 3)
-    line.start_scatter(image_parts, image_slots, 2, part=slice(1, None))
-    plane.start_scatter(text_parts, text_slots, 2, ascending, slice(pair_count, None))
+    line.wait_some(image_parts, 2, 1)
+    line.start_scatter(image_parts, image_slots, 2, part=slice(1, None), later=4)
+    plane.start_scatter(text_parts, text_slots, 2, ascending, slice(pair_count, None), 6)
 
     rows = image_ref.shape[0]
     plane.wait_recv(text_slots, 2)
@@ -299,6 +279,9 @@
     examples = 2.0 * line.size * plane.size * rows
     whole = jnp.sum(row_sums[...], axis=0)[0:1, 0:1] + jnp.sum(col_sums[...], axis=0)[0:1, 0:1]
     loss_ref[...] = jnp.broadcast_to(whole / examples, loss_ref.shape)
+    plane.wait_some(text_parts, 2, pair_count)
+    line.wait_some(image_parts, 4, line_count - 2)
+    plane.wait_some(text_parts, 6, plane.size - 1 - pair_count)
     line.wait_send(images, 0)
     some(near_blocks, 0).wait_send()
     if far:
@@ -306,7 +289,6 @@
         some(len(far), 5).wait_send()
     for buf_line, buf_plane, stage in (
         (row_stats, col_stats, 1),
-        (image_parts, text_parts, 2),
         (col_sums, row_sums, 3),
     ):
         line.wait_send(buf_line, stage)
@@ -355,11 +337,10 @@
                 pltpu.VMEM((rows, width), jnp.float32),
                 pltpu.VMEM((rows, width), jnp.float32),
                 pltpu.SemaphoreType.DMA((2,)),
-                pltpu.SemaphoreType.DMA((4,)),
-                pltpu.SemaphoreType.DMA((4,)),
-                pltpu.SemaphoreType.DMA((6,)),
-                pltpu.SemaphoreType.DMA((6,)),
-                pltpu.SemaphoreType.REGULAR,
+                pltpu.SemaphoreType.DMA((5,)),
+                pltpu.SemaphoreType.DMA((5,)),
+                pltpu.SemaphoreType.DMA((7,)),
+                pltpu.SemaphoreType.DMA((7,)),
             ],
             compiler_params=pltpu.CompilerParams(
                 collective_id=0, has_side_effects=True, vmem_limit_bytes=56 * 1024 * 1024

time: 22.1 us -> 21.7 us (0.982)
  Pallas kernels: 20.6 us -> 20.3 us
    pallas_call x1, Pallas kernels: 19.9 us -> 19.6 us  [on_device(): pl.pallas_call(functools.partial(kernel, inner_count, line_count, pair_co...]
where the time goes in v4:
time: 21.7 us; the launch traced here: 21.5 us
  Pallas kernels  20.3 us (94%)
  between operations  1.28 us (6%)
    pallas_call x1, Pallas kernels, on_device(): pl.pallas_call(functools.partial(kernel, inner_count, line_count, pair_co...  19.6 us
    pallas_call x1, Pallas kernels, on_device(): pl.pallas_call(store, out_shape=(jax.ShapeDtypeStruct((1, 128), jnp.float...  0.69 us

profile of v4, /device:TPU:0, one launch (start us, length us, event | category | flops | bytes accessed | tf_op | source)
XLA Modules:
  0.0 21.5 jit_solution(12804617491156734909)
XLA Ops:
  1.3 19.6 %contrastive.1 = (f32[1,128]{1,0:T(1,128)S(1)}, f32[24,768]{1,0:T(8,128)S(1)}, f32[24,768]{1,0:T(8,128)S(1)}) custom-call(f32[1]{0:T(128)S(6)} %copy.6.scale_ref, f32[24,768]{1,0:T(8,128)} %image_hbm.1, f32[24,768]{1,0:T(8,128)} %text_hbm.1), custom_call_target="tpu_custom_call" | custom-call | tf_op jit(solution)/shard_map/contrastive/pallas_call | solution.py:319
  20.9 0.7 %store.1 = (f32[1,128]{1,0:T(1,128)}, f32[24,768]{1,0:T(8,128)}, f32[24,768]{1,0:T(8,128)}) custom-call(f32[1,128]{1,0:T(1,128)S(1)} %get-tuple-element.9.loss, f32[24,768]{1,0:T(8,128)S(1)} %get-tuple-element.10.image_grad, f32[24,768]{1,0:T(8,128)S(1)} %get-tuple-element.11.text_grad), custom_call_target="tpu_custom_call" | custom-call | tf_op jit(solution)/shard_map/store/pallas_call | solution.py:351

commit v5 on v4

--- a/solution.py
+++ b/solution.py
@@ -133,8 +133,6 @@
     text_parts,
     image_slots,
     text_slots,
-    image_own,
-    text_own,
     image_ref,
     text_ref,
     input_sems,
@@ -220,37 +218,47 @@
     image_group = flat_half(images[...])
     text_group = flat_half(texts[...])
     image_count, text_count = image_group.shape[0], text_group.shape[0]
+    turned_logits = factor * lax.dot_general(
+        text_group, image_group, (((1,), (1,)), ((), ())), preferred_element_type=jnp.float32
+    )
+    row_peak = jnp.max(turned_logits, axis=0, keepdims=True)
+    row_total = jnp.sum(jnp.exp(turned_logits - row_peak), axis=0, keepdims=True)
+    row_stats[line.me, 0:1, :] = row_peak
+    row_stats[line.me, 1:2, :] = row_total
+    line.start_gather(row_stats, 1, far_first)
     logits = factor * lax.dot_general(
         image_group, text_group, (((1,), (1,)), ((), ())), preferred_element_type=jnp.float32
     )
-    row_peak = jnp.max(logits, axis=1, keepdims=True)
-    row_total = jnp.sum(jnp.exp(logits - row_peak), axis=1, keepdims=True)
     col_peak = jnp.max(logits, axis=0, keepdims=True)
     col_total = jnp.sum(jnp.exp(logits - col_peak), axis=0, keepdims=True)
-    row_stats[line.me, 0:1, :] = as_row(row_peak)
-    row_stats[line.me, 1:2, :] = as_row(row_total)
     col_stats[plane.me, 0:1, :] = col_peak
     col_stats[plane.me, 1:2, :] = col_total
     col_stats[plane.me, 2:3, :] = jnp.full((1, text_count), diagonal, jnp.float32)
-    line.start_gather(row_stats, 1)
     plane.start_gather(col_stats, 1)
+    plane.wait_recv(col_stats, 1)
+    col_lse = merge(col_stats[...])
+    col_weights = jnp.exp(logits - col_lse)
+    turned_weights = jnp.exp(turned_logits - as_column(col_lse))
     line.wait_recv(row_stats, 1)
-    plane.wait_recv(col_stats, 1)
     row_lse = merge(row_stats[...])
-    col_lse = merge(col_stats[...])
 
     weights = (
-        0.5 * factor * (jnp.exp(logits - as_column(row_lse)) + jnp.exp(logits - col_lse))
+        0.5 * factor * (jnp.exp(logits - as_column(row_lse)) + col_weights)
     ).astype(jnp.bfloat16)
-    image_own[...] = jnp.dot(
-        weights, text_group, preferred_element_type=jnp.float32
-    ).reshape(image_parts.shape)
-    image_parts[...] = image_own[...].astype(jnp.bfloat16)
+    image_parts[...] = (
+        jnp.dot(weights, text_group, preferred_element_type=jnp.float32)
+        .reshape(image_parts.shape)
+        .astype(jnp.bfloat16)
+    )
     line.start_scatter(image_parts, image_slots, 2, part=slice(0, 1))
-    text_own[...] = lax.dot_general(
-        weights, image_group, (((0,), (0,)), ((), ())), preferred_element_type=jnp.float32
-    ).reshape(text_parts.shape)
-    text_parts[...] = text_own[...].astype(jnp.bfloat16)
+    turned_weights = (
+        0.5 * factor * (jnp.exp(turned_logits - row_lse) + turned_weights)
+    ).astype(jnp.bfloat16)
+    text_parts[...] = (
+        jnp.dot(turned_weights, image_group, preferred_element_type=jnp.float32)
+        .reshape(text_parts.shape)
+        .astype(jnp.bfloat16)
+    )
     plane.start_scatter(text_parts, text_slots, 2, ascending, slice(0, pair_count))
     tile = row_sums.shape[1:]
     plane_diagonal = jnp.sum(col_stats[:, 2, 0:1])
@@ -264,12 +272,12 @@
 
     rows = image_ref.shape[0]
     plane.wait_recv(text_slots, 2)
-    text_sum = text_own[plane.me]
+    text_sum = text_parts[plane.me].astype(jnp.float32)
     for other in plane.others():
         text_sum = text_sum + text_slots[other].astype(jnp.float32)
     text_grad_ref[...] = project(text_sum - factor * image_back, text_unit, text_inverse)
     line.wait_recv(image_slots, 2)
-    image_sum = image_own[line.me]
+    image_sum = image_parts[line.me].astype(jnp.float32)
     for other in line.others():
         image_sum = image_sum + image_slots[other].astype(jnp.float32)
     image_grad_ref[...] = project(image_sum - factor * text_back, image_unit, image_inverse)
@@ -332,8 +340,6 @@
                 pltpu.VMEM((plane_count, rows, width), jnp.bfloat16),
                 pltpu.VMEM((line_count, rows, width), jnp.bfloat16),
                 pltpu.VMEM((plane_count, rows, width), jnp.bfloat16),
-                pltpu.VMEM((line_count, rows, width), jnp.float32),
-                pltpu.VMEM((plane_count, rows, width), jnp.float32),
                 pltpu.VMEM((rows, width), jnp.float32),
                 pltpu.VMEM((rows, width), jnp.float32),
                 pltpu.SemaphoreType.DMA((2,)),

time: 21.7 us -> 21.5 us (level)
  no operation moved by 1% of the time
where the time goes in v5:
time: 21.5 us; the launch traced here: 21.3 us
  Pallas kernels  20.1 us (93%)
  between operations  1.28 us (6%)
    pallas_call x1, Pallas kernels, on_device(): pl.pallas_call(functools.partial(kernel, inner_count, line_count, pair_co...  19.4 us
    pallas_call x1, Pallas kernels, on_device(): pl.pallas_call(store, out_shape=(jax.ShapeDtypeStruct((1, 128), jnp.float...  0.69 us

profile of v5, /device:TPU:0, one launch (start us, length us, event | category | flops | bytes accessed | tf_op | source)
XLA Modules:
  0.0 21.3 jit_solution(12369154738321626430)
XLA Ops:
  1.3 19.4 %contrastive.1 = (f32[1,128]{1,0:T(1,128)S(1)}, f32[24,768]{1,0:T(8,128)S(1)}, f32[24,768]{1,0:T(8,128)S(1)}) custom-call(f32[1]{0:T(128)S(6)} %copy.6.scale_ref, f32[24,768]{1,0:T(8,128)} %image_hbm.1, f32[24,768]{1,0:T(8,128)} %text_hbm.1), custom_call_target="tpu_custom_call" | custom-call | tf_op jit(solution)/shard_map/contrastive/pallas_call | solution.py:327
  20.7 0.7 %store.1 = (f32[1,128]{1,0:T(1,128)}, f32[24,768]{1,0:T(8,128)}, f32[24,768]{1,0:T(8,128)}) custom-call(f32[1,128]{1,0:T(1,128)S(1)} %get-tuple-element.9.loss, f32[24,768]{1,0:T(8,128)S(1)} %get-tuple-element.10.image_grad, f32[24,768]{1,0:T(8,128)S(1)} %get-tuple-element.11.text_grad), custom_call_target="tpu_custom_call" | custom-call | tf_op jit(solution)/shard_map/store/pallas_call | solution.py:357

commit v6 on v5

--- a/solution.py
+++ b/solution.py
@@ -182,7 +182,7 @@
     slot = lambda g, c: texts.at[g * pair_count + c]
 
     def text_copy(block, g, c, stage):
-        return plane.copy(block, block, stage, g * pair_count + c)
+        return plane.copy(block, block, stage, g * pair_count + c, 0)
 
     def start_texts():
         mine = slot(inner, side)
@@ -211,12 +211,12 @@
         for k in far:
             text_copy(slot(chip_at(k), side), inner, 1 - side, 5).start()
     some(near_blocks, 0).wait_recv()
-    line.wait_recv(images, 0)
     if far:
         some(len(far), 5).wait_recv()
+    text_group = flat_half(texts[...])
+    line.wait_recv(images, 0)
 
     image_group = flat_half(images[...])
-    text_group = flat_half(texts[...])
     image_count, text_count = image_group.shape[0], text_group.shape[0]
     turned_logits = factor * lax.dot_general(
         text_group, image_group, (((1,), (1,)), ((), ())), preferred_element_type=jnp.float32
@@ -268,7 +268,7 @@
     line.start_gather(col_sums, 3)
     line.wait_some(image_parts, 2, 1)
     line.start_scatter(image_parts, image_slots, 2, part=slice(1, None), later=4)
-    plane.start_scatter(text_parts, text_slots, 2, ascending, slice(pair_count, None), 6)
+    plane.start_scatter(text_parts, text_slots, 2, ascending, slice(pair_count, None), 4)
 
     rows = image_ref.shape[0]
     plane.wait_recv(text_slots, 2)
@@ -289,12 +289,9 @@
     loss_ref[...] = jnp.broadcast_to(whole / examples, loss_ref.shape)
     plane.wait_some(text_parts, 2, pair_count)
     line.wait_some(image_parts, 4, line_count - 2)
-    plane.wait_some(text_parts, 6, plane.size - 1 - pair_count)
+    plane.wait_some(text_parts, 4, plane.size - 1 - pair_count)
     line.wait_send(images, 0)
-    some(near_blocks, 0).wait_send()
-    if far:
-        some(len(far), 4).wait_send()
-        some(len(far), 5).wait_send()
+    some(near_blocks + 2 * len(far), 0).wait_send()
     for buf_line, buf_plane, stage in (
         (row_stats, col_stats, 1),
         (col_sums, row_sums, 3),
@@ -344,9 +341,9 @@
                 pltpu.VMEM((rows, width), jnp.float32),
                 pltpu.SemaphoreType.DMA((2,)),
                 pltpu.SemaphoreType.DMA((5,)),
+                pltpu.SemaphoreType.DMA((4,)),
                 pltpu.SemaphoreType.DMA((5,)),
-                pltpu.SemaphoreType.DMA((7,)),
-                pltpu.SemaphoreType.DMA((7,)),
+                pltpu.SemaphoreType.DMA((6,)),
             ],
             compiler_params=pltpu.CompilerParams(
                 collective_id=0, has_side_effects=True, vmem_limit_bytes=56 * 1024 * 1024

time: 21.5 us -> 21.5 us (level)
  no operation moved by 1% of the time
where the time goes in v6:
time: 21.5 us; the launch traced here: 21.3 us
  Pallas kernels  20 us (93%)
  between operations  1.28 us (6%)
    pallas_call x1, Pallas kernels, on_device(): pl.pallas_call(functools.partial(kernel, inner_count, line_count, pair_co...  19.4 us
    pallas_call x1, Pallas kernels, on_device(): pl.pallas_call(store, out_shape=(jax.ShapeDtypeStruct((1, 128), jnp.float...  0.69 us

profile of v6, /device:TPU:0, one launch (start us, length us, event | category | flops | bytes accessed | tf_op | source)
XLA Modules:
  0.0 21.3 jit_solution(13900060700099578904)
XLA Ops:
  1.3 19.4 %contrastive.1 = (f32[1,128]{1,0:T(1,128)S(1)}, f32[24,768]{1,0:T(8,128)S(1)}, f32[24,768]{1,0:T(8,128)S(1)}) custom-call(f32[1]{0:T(128)S(6)} %copy.6.scale_ref, f32[24,768]{1,0:T(8,128)} %image_hbm.1, f32[24,768]{1,0:T(8,128)} %text_hbm.1), custom_call_target="tpu_custom_call" | custom-call | tf_op jit(solution)/shard_map/contrastive/pallas_call | solution.py:324
  20.6 0.7 %store.1 = (f32[1,128]{1,0:T(1,128)}, f32[24,768]{1,0:T(8,128)}, f32[24,768]{1,0:T(8,128)}) custom-call(f32[1,128]{1,0:T(1,128)S(1)} %get-tuple-element.9.loss, f32[24,768]{1,0:T(8,128)S(1)} %get-tuple-element.10.image_grad, f32[24,768]{1,0:T(8,128)S(1)} %get-tuple-element.11.text_grad), custom_call_target="tpu_custom_call" | custom-call | tf_op jit(solution)/shard_map/store/pallas_call | solution.py:354

commit v7 on v6

--- a/solution.py
+++ b/solution.py
@@ -266,7 +266,13 @@
     col_sums[line.me] = jnp.full(tile, jnp.sum(col_lse) - 2.0 * plane_diagonal, jnp.float32)
     plane.start_gather(row_sums, 3)
     line.start_gather(col_sums, 3)
-    line.wait_some(image_parts, 2, 1)
+
+    held = place == line_count - 1
+
+    @pl.when(held)
+    def _():
+        line.wait_some(image_parts, 2, 1)
+
     line.start_scatter(image_parts, image_slots, 2, part=slice(1, None), later=4)
     plane.start_scatter(text_parts, text_slots, 2, ascending, slice(pair_count, None), 4)
 
@@ -288,6 +294,11 @@
     whole = jnp.sum(row_sums[...], axis=0)[0:1, 0:1] + jnp.sum(col_sums[...], axis=0)[0:1, 0:1]
     loss_ref[...] = jnp.broadcast_to(whole / examples, loss_ref.shape)
     plane.wait_some(text_parts, 2, pair_count)
+
+    @pl.when(jnp.logical_not(held))
+    def _():
+        line.wait_some(image_parts, 2, 1)
+
     line.wait_some(image_parts, 4, line_count - 2)
     plane.wait_some(text_parts, 4, plane.size - 1 - pair_count)
     line.wait_send(images, 0)

time: 21.5 us -> 21.5 us (level)
  no operation moved by 1% of the time
where the time goes in v7:
time: 21.5 us; the launch traced here: 21.3 us
  Pallas kernels  20.1 us (93%)
  between operations  1.28 us (6%)
    pallas_call x1, Pallas kernels, on_device(): pl.pallas_call(functools.partial(kernel, inner_count, line_count, pair_co...  19.4 us
    pallas_call x1, Pallas kernels, on_device(): pl.pallas_call(store, out_shape=(jax.ShapeDtypeStruct((1, 128), jnp.float...  0.69 us

profile of v7, /device:TPU:0, one launch (start us, length us, event | category | flops | bytes accessed | tf_op | source)
XLA Modules:
  0.0 21.3 jit_solution(3238230038036221597)
XLA Ops:
  1.3 19.4 %contrastive.1 = (f32[1,128]{1,0:T(1,128)S(1)}, f32[24,768]{1,0:T(8,128)S(1)}, f32[24,768]{1,0:T(8,128)S(1)}) custom-call(f32[1]{0:T(128)S(6)} %copy.6.scale_ref, f32[24,768]{1,0:T(8,128)} %image_hbm.1, f32[24,768]{1,0:T(8,128)} %text_hbm.1), custom_call_target="tpu_custom_call" | custom-call | tf_op jit(solution)/shard_map/contrastive/pallas_call | solution.py:335
  20.6 0.7 %store.1 = (f32[1,128]{1,0:T(1,128)}, f32[24,768]{1,0:T(8,128)}, f32[24,768]{1,0:T(8,128)}) custom-call(f32[1,128]{1,0:T(1,128)S(1)} %get-tuple-element.9.loss, f32[24,768]{1,0:T(8,128)S(1)} %get-tuple-element.10.image_grad, f32[24,768]{1,0:T(8,128)S(1)} %get-tuple-element.11.text_grad), custom_call_target="tpu_custom_call" | custom-call | tf_op jit(solution)/shard_map/store/pallas_call | solution.py:365

commit v8 on v7

--- a/solution.py
+++ b/solution.py
@@ -277,16 +277,16 @@
     plane.start_scatter(text_parts, text_slots, 2, ascending, slice(pair_count, None), 4)
 
     rows = image_ref.shape[0]
+    line.wait_recv(image_slots, 2)
+    image_sum = image_parts[line.me].astype(jnp.float32)
+    for other in line.others():
+        image_sum = image_sum + image_slots[other].astype(jnp.float32)
+    image_grad_ref[...] = project(image_sum - factor * text_back, image_unit, image_inverse)
     plane.wait_recv(text_slots, 2)
     text_sum = text_parts[plane.me].astype(jnp.float32)
     for other in plane.others():
         text_sum = text_sum + text_slots[other].astype(jnp.float32)
     text_grad_ref[...] = project(text_sum - factor * image_back, text_unit, text_inverse)
-    line.wait_recv(image_slots, 2)
-    image_sum = image_parts[line.me].astype(jnp.float32)
-    for other in line.others():
-        image_sum = image_sum + image_slots[other].astype(jnp.float32)
-    image_grad_ref[...] = project(image_sum - factor * text_back, image_unit, image_inverse)
 
     plane.wait_recv(row_sums, 3)
     line.wait_recv(col_sums, 3)

time: 21.5 us -> 21.6 us (level)
  no operation moved by 1% of the time
where the time goes in v8:
time: 21.6 us; the launch traced here: 21.4 us
  Pallas kernels  20.1 us (93%)
  between operations  1.28 us (6%)
    pallas_call x1, Pallas kernels, on_device(): pl.pallas_call(functools.partial(kernel, inner_count, line_count, pair_co...  19.4 us
    pallas_call x1, Pallas kernels, on_device(): pl.pallas_call(store, out_shape=(jax.ShapeDtypeStruct((1, 128), jnp.float...  0.69 us

profile of v8, /device:TPU:0, one launch (start us, length us, event | category | flops | bytes accessed | tf_op | source)
XLA Modules:
  0.0 21.4 jit_solution(14078991980378941937)
XLA Ops:
  1.3 19.4 %contrastive.1 = (f32[1,128]{1,0:T(1,128)S(1)}, f32[24,768]{1,0:T(8,128)S(1)}, f32[24,768]{1,0:T(8,128)S(1)}) custom-call(f32[1]{0:T(128)S(6)} %copy.6.scale_ref, f32[24,768]{1,0:T(8,128)} %image_hbm.1, f32[24,768]{1,0:T(8,128)} %text_hbm.1), custom_call_target="tpu_custom_call" | custom-call | tf_op jit(solution)/shard_map/contrastive/pallas_call | solution.py:335
  20.7 0.7 %store.1 = (f32[1,128]{1,0:T(1,128)}, f32[24,768]{1,0:T(8,128)}, f32[24,768]{1,0:T(8,128)}) custom-call(f32[1,128]{1,0:T(1,128)S(1)} %get-tuple-element.9.loss, f32[24,768]{1,0:T(8,128)S(1)} %get-tuple-element.10.image_grad, f32[24,768]{1,0:T(8,128)S(1)} %get-tuple-element.11.text_grad), custom_call_target="tpu_custom_call" | custom-call | tf_op jit(solution)/shard_map/store/pallas_call | solution.py:365

commit v9 on v7

--- a/solution.py
+++ b/solution.py
@@ -242,6 +242,13 @@
     line.wait_recv(row_stats, 1)
     row_lse = merge(row_stats[...])
 
+    tile = row_sums.shape[1:]
+    plane_diagonal = jnp.sum(col_stats[:, 2, 0:1])
+    row_sums[plane.me] = jnp.full(tile, jnp.sum(row_lse), jnp.float32)
+    col_sums[line.me] = jnp.full(tile, jnp.sum(col_lse) - 2.0 * plane_diagonal, jnp.float32)
+    plane.start_gather(row_sums, 3)
+    line.start_gather(col_sums, 3)
+
     weights = (
         0.5 * factor * (jnp.exp(logits - as_column(row_lse)) + col_weights)
     ).astype(jnp.bfloat16)
@@ -260,13 +267,6 @@
         .astype(jnp.bfloat16)
     )
     plane.start_scatter(text_parts, text_slots, 2, ascending, slice(0, pair_count))
-    tile = row_sums.shape[1:]
-    plane_diagonal = jnp.sum(col_stats[:, 2, 0:1])
-    row_sums[plane.me] = jnp.full(tile, jnp.sum(row_lse), jnp.float32)
-    col_sums[line.me] = jnp.full(tile, jnp.sum(col_lse) - 2.0 * plane_diagonal, jnp.float32)
-    plane.start_gather(row_sums, 3)
-    line.start_gather(col_sums, 3)
-
     held = place == line_count - 1
 
     @pl.when(held)

time: 21.5 us -> 21.4 us (level)
  no operation moved by 1% of the time
where the time goes in v9:
time: 21.4 us; the launch traced here: 21.3 us
  Pallas kernels  20 us (93%)
  between operations  1.28 us (6%)
    pallas_call x1, Pallas kernels, on_device(): pl.pallas_call(functools.partial(kernel, inner_count, line_count, pair_co...  19.3 us
    pallas_call x1, Pallas kernels, on_device(): pl.pallas_call(store, out_shape=(jax.ShapeDtypeStruct((1, 128), jnp.float...  0.69 us

profile of v9, /device:TPU:0, one launch (start us, length us, event | category | flops | bytes accessed | tf_op | source)
XLA Modules:
  0.0 21.3 jit_solution(5434606936730917926)
XLA Ops:
  1.3 19.3 %contrastive.1 = (f32[1,128]{1,0:T(1,128)S(1)}, f32[24,768]{1,0:T(8,128)S(1)}, f32[24,768]{1,0:T(8,128)S(1)}) custom-call(f32[1]{0:T(128)S(6)} %copy.6.scale_ref, f32[24,768]{1,0:T(8,128)} %image_hbm.1, f32[24,768]{1,0:T(8,128)} %text_hbm.1), custom_call_target="tpu_custom_call" | custom-call | tf_op jit(solution)/shard_map/contrastive/pallas_call | solution.py:335
  20.6 0.7 %store.1 = (f32[1,128]{1,0:T(1,128)}, f32[24,768]{1,0:T(8,128)}, f32[24,768]{1,0:T(8,128)}) custom-call(f32[1,128]{1,0:T(1,128)S(1)} %get-tuple-element.9.loss, f32[24,768]{1,0:T(8,128)S(1)} %get-tuple-element.10.image_grad, f32[24,768]{1,0:T(8,128)S(1)} %get-tuple-element.11.text_grad), custom_call_target="tpu_custom_call" | custom-call | tf_op jit(solution)/shard_map/store/pallas_call | solution.py:365
